TPU v7x, 256 devices: a whole 4x4x8 slice. The times are simulated.
256 devices in a mesh: ctx: 32 (over z, x_lo, core), head: 8 (over x_hi, y).
Axes of the slice: x: 4 (x_hi: 2, x_lo: 2; x = x_hi * 2 + x_lo), y: 4, z: 8, core: 2. Of those that a mesh axis runs over, the one named last changes fastest.
Arguments:
- queries: bfloat16 [8192, 24, 128], P('ctx', 'head'), may hold values from -4.5 to 4.5, as said below
- key_vectors: bfloat16 [8192, 24, 128], P('ctx', 'head'), may hold values from -4.5 to 4.5, as said below
- value_vectors: bfloat16 [8192, 24, 128], P('ctx', 'head'), may hold values from -6 to 6
- attn_output: bfloat16 [8192, 24, 128], P('ctx', 'head'), may hold values from -6 to 6
- output_grad: bfloat16 [8192, 5120], P('ctx', 'head'), may hold values from -6 to 6
- w_out: bfloat16 [3072, 5120], P('head'), may hold values from -0.078125 to 0.078125
- log_total: float32 [8192, 24], P('ctx', 'head'), as said below
Outputs:
- query_grad: bfloat16 [8192, 24, 128], P('ctx', 'head')
- key_grad: bfloat16 [8192, 24, 128], P('ctx', 'head')
- value_grad: bfloat16 [8192, 24, 128], P('ctx', 'head')
Inputs may be any that keep to these rules, and one draw needn't show every extreme that they name: `queries`: independent entries of order one. `key_vectors`: entries of order one. `log_total`: for each position and head, the log of the sum of exp(scores) over the positions it sees, from the given queries and keys.
All inputs are finite; a program needn't handle non-finite values.
Results may differ from a plain program's by a relative error of at most 0.0058.
Values may be sent and summed in bfloat16 or wider, within the bound.
A program may use at most 128 MiB of HBM per device.

v0:
```python
import jax
import jax.numpy as jnp
from jax import lax
from jax.sharding import PartitionSpec as P


def block_terms(
    query_block,
    grad_block,
    total_block,
    delta_block,
    key_block,
    value_block,
    query_pos,
    key_pos,
    factor,
):
    raw_scores = (
        jnp.einsum("qhd,khd->hqk", query_block, key_block, preferred_element_type=jnp.float32)
        * factor
    )
    visible = key_pos[None, None, :] <= query_pos[None, :, None]
    scores = jnp.where(visible, raw_scores, -jnp.inf)
    prob_full = jnp.exp(scores - total_block[:, :, None])
    prob_grad = jnp.einsum(
        "qhd,khd->hqk", grad_block, value_block, preferred_element_type=jnp.float32
    )
    score_grad = (prob_full * (prob_grad - delta_block[:, :, None])).astype(jnp.bfloat16)
    return (prob_full.astype(jnp.bfloat16), score_grad)


def query_pass(query_group, gathered_keys, gathered_values, span_rows, factor):
    query_rows, grad_rows, total_rows, delta_rows, query_pos = query_group
    highest = jnp.max(query_pos)

    def query_advance(step_index, running):
        offset = step_index * span_rows

        def query_update(query_grad):
            key_block = lax.dynamic_slice_in_dim(gathered_keys, offset, span_rows, 0)
            value_block = lax.dynamic_slice_in_dim(gathered_values, offset, span_rows, 0)
            key_pos = offset + jnp.arange(span_rows, dtype=jnp.int32)
            prob_low, score_grad = block_terms(
                query_rows,
                grad_rows,
                total_rows,
                delta_rows,
                key_block,
                value_block,
                query_pos,
                key_pos,
                factor,
            )
            return (
                query_grad
                + jnp.einsum(
                    "hqk,khd->qhd", score_grad, key_block, preferred_element_type=jnp.float32
                )
                * factor
            )

        return lax.cond(offset <= highest, query_update, lambda carried: carried, running)

    initial = jnp.zeros(query_rows.shape, jnp.float32)
    return lax.fori_loop(0, gathered_keys.shape[0] // span_rows, query_advance, initial)


def key_pass(
    own_keys, own_values, key_pos, all_queries, all_grads, all_totals, all_deltas, span_rows, factor
):
    lowest = jnp.min(key_pos)

    def key_advance(step_index, running):
        offset = step_index * span_rows

        def key_update(carried):
            key_grad, value_grad = carried
            query_block = lax.dynamic_slice_in_dim(all_queries, offset, span_rows, 0)
            grad_block = lax.dynamic_slice_in_dim(all_grads, offset, span_rows, 0)
            total_block = lax.dynamic_slice_in_dim(all_totals, offset, span_rows, 1)
            delta_block = lax.dynamic_slice_in_dim(all_deltas, offset, span_rows, 1)
            query_pos = offset + jnp.arange(span_rows, dtype=jnp.int32)
            prob_low, score_grad = block_terms(
                query_block,
                grad_block,
                total_block,
                delta_block,
                own_keys,
                own_values,
                query_pos,
                key_pos,
                factor,
            )
            key_grad = (
                key_grad
                + jnp.einsum(
                    "hqk,qhd->khd", score_grad, query_block, preferred_element_type=jnp.float32
                )
                * factor
            )
            value_grad = value_grad + jnp.einsum(
                "hqk,qhd->khd", prob_low, grad_block, preferred_element_type=jnp.float32
            )
            return (key_grad, value_grad)

        return lax.cond(
            offset + span_rows - 1 >= lowest, key_update, lambda carried: carried, running
        )

    initial = (jnp.zeros(own_keys.shape, jnp.float32), jnp.zeros(own_values.shape, jnp.float32))
    return lax.fori_loop(0, all_queries.shape[0] // span_rows, key_advance, initial)


def body(queries, key_vectors, value_vectors, attn_output, output_grad, w_out, log_total):
    local_rows, head_count, head_width = queries.shape
    factor = head_width ** (-0.5)
    ctx_count = lax.axis_size("ctx")
    ctx_index = lax.axis_index("ctx")
    total_len = local_rows * ctx_count
    span_rows = min(512, total_len)
    grad_flat = jnp.einsum(
        "tc,rc->tr",
        lax.all_gather(output_grad, "head", axis=1, tiled=True),
        w_out,
        preferred_element_type=jnp.float32,
    )
    attn_grad = grad_flat.astype(jnp.bfloat16).reshape(local_rows, head_count, head_width)
    row_delta = jnp.einsum(
        "qhd,qhd->hq", attn_grad, attn_output, preferred_element_type=jnp.float32
    )
    own_total = jnp.transpose(log_total, (1, 0))
    own_pos = ctx_index * local_rows + jnp.arange(local_rows, dtype=jnp.int32)
    groups = [(queries, attn_grad, own_total, row_delta, own_pos)]
    gathered_keys, gathered_values = (
        lax.all_gather(key_vectors, "ctx", axis=0, tiled=True),
        lax.all_gather(value_vectors, "ctx", axis=0, tiled=True),
    )
    partial_grads = [
        query_pass(query_group, gathered_keys, gathered_values, span_rows, factor)
        for query_group in groups
    ]
    all_queries, all_grads = (
        lax.all_gather(queries, "ctx", axis=0, tiled=True),
        lax.all_gather(attn_grad, "ctx", axis=0, tiled=True),
    )
    all_totals, all_deltas = (
        lax.all_gather(own_total, "ctx", axis=1, tiled=True),
        lax.all_gather(row_delta, "ctx", axis=1, tiled=True),
    )
    key_part, value_part = key_pass(
        key_vectors,
        value_vectors,
        own_pos,
        all_queries,
        all_grads,
        all_totals,
        all_deltas,
        span_rows,
        factor,
    )
    results = [piece.astype(jnp.bfloat16) for piece in partial_grads]
    query_grad = results[0]
    return (query_grad, key_part.astype(jnp.bfloat16), value_part.astype(jnp.bfloat16))


def solution(mesh):
    in_specs = (
        P("ctx", "head", None),
        P("ctx", "head", None),
        P("ctx", "head", None),
        P("ctx", "head", None),
        P("ctx", "head"),
        P("head", None),
        P("ctx", "head"),
    )
    out_specs = (P("ctx", "head", None), P("ctx", "head", None), P("ctx", "head", None))
    return jax.shard_map(body, mesh=mesh, in_specs=in_specs, out_specs=out_specs, check_vma=False)
```

profile of v0, /device:TPU:1, one launch (start us, length us, event | category | flops | bytes accessed | tf_op | source)
XLA Modules:
  0.0 466.0 jit_solution(10017530869229409577)
XLA Ops:
  9.4 67.1 %all-gather.10.cloned.1.call-done = bf16[256,5120]{1,0:T(8,128)(2,1)} async-done(((bf16[256,640]{1,0:T(8,128)(2,1)}), bf16[256,5120]{1,0:T(8,128)(2,1)}) %all-gather.10.cloned.1.call-update) | async-done | bytes 2621456 | tf_op jit(solution)/shard_map/all_gather | solution.py:123
  76.6 4.4 convolution_convert_fusion
  83.8 35.6 %all_gather.25 = f32[3,8192]{1,0:T(4,128)S(1)} all-gather(f32[3,256]{1,0:T(4,128)S(1)} %bitcast.56), channel_id=1, replica_groups=mesh['ctx'=32,'head'=8] {'ctx'}, dimensions={1}, use_global_device_ids=true | all-gather | bytes 101376 | tf_op jit(solution)/shard_map/all_gather | solution.py:147
  121.8 31.2 %all_gather.27 = f32[3,8192]{1,0:T(4,128)S(1)} all-gather(f32[3,256]{1,0:T(4,128)S(1)} %multiply_reduce_fusion), channel_id=1, replica_groups=mesh['ctx'=32,'head'=8] {'ctx'}, dimensions={1}, use_global_device_ids=true | all-gather | bytes 101376 | tf_op jit(solution)/shard_map/all_gather | solution.py:148
  153.0 64.4 %all-gather.8.cloned.1.call-done = bf16[8192,3,128]{2,0,1:T(8,128)(2,1)} async-done(((bf16[256,3,128]{2,0,1:T(8,128)(2,1)}), bf16[8192,3,128]{2,0,1:T(8,128)(2,1)}) %all-gather.8.cloned.1.call-update) | async-done | bytes 6291472 | tf_op jit(solution)/shard_map/all_gather | solution.py:136
  217.4 14.6 %while.37 = (s32[]{:T(128)}, f32[256,3,128]{0,2,1:T(8,128)S(1)}, s32[]{:T(128)}, bf16[8192,3,128]{2,0,1:T(8,128)(2,1)}, bf16[256,3,128]{2,0,1:T(8,128)(2,1)S(1)}...) while((s32[]{:T(128)}, f32[256,3,128]{0,2,1:T(8,128)S(1)}, ...), condition=%wide.region_4.5_spmd.clone, body=%wide.region_1.4_spmd.clone.sunk | while | flops 304677632 | bytes 5782805 | solution.py:65
  218.1 3.5 conditional.6
  219.7 2.0 fusion.10
  232.9 66.2 %all-gather.14.cloned.1.call-done = bf16[8192,3,128]{0,2,1:T(8,128)(2,1)} async-done(((bf16[256,3,128]{0,2,1:T(8,128)(2,1)}), bf16[8192,3,128]{0,2,1:T(8,128)(2,1)}) %all-gather.14.cloned.1.call-update) | async-done | bytes 6291472 | tf_op jit(solution)/shard_map/all_gather | solution.py:144
  299.1 8.6 %copy.36 = bf16[8192,3,128]{2,0,1:T(8,128)(2,1)} copy(bf16[8192,3,128]{0,2,1:T(8,128)(2,1)} %all-gather.14.cloned.1.call-done) | data formatting | bytes 12582912
  307.7 60.7 %all-gather.12.cloned.1.call-done = bf16[8192,3,128]{2,0,1:T(8,128)(2,1)} async-done(((bf16[256,3,128]{2,0,1:T(8,128)(2,1)}), bf16[8192,3,128]{2,0,1:T(8,128)(2,1)}) %all-gather.12.cloned.1.call-update) | async-done | bytes 6291472 | tf_op jit(solution)/shard_map/all_gather | solution.py:143
  368.5 89.4 %while.38 = (s32[]{:T(128)}, f32[256,3,128]{0,2,1:T(8,128)S(1)}, f32[256,3,128]{0,2,1:T(8,128)S(1)}, s32[]{:T(128)}, bf16[8192,3,128]{2,0,1:T(8,128)(2,1)}, /*in...) while((s32[]{:T(128)}, f32[256,3,128]{0,2,1:T(8,128)S(1)}, ...), condition=%wide.region_9.10_spmd.clone, body=%wide.region_6.9_spmd.clone.sunk | while | flops 405832448 | bytes 8566113 | solution.py:111
  369.1 4.9 %conditional.7 = ((f32[256,3,128]{0,2,1:T(8,128)S(1)}, f32[256,3,128]{0,2,1:T(8,128)S(1)})) conditional(s32[]{:T(128)} %convert_element_type.71, (f32[256,3,128]{0,2,1:T(8,128)S(1)}, f32[256,3,128]{0,2,1:T(8,128)S(1)}) %tuple.108, (s32[]{:T(128)}, bf16[8192,3,128]{2,0,1:T(8,128)(2,1)}, s32[]{:T(128)}, bf16[256,3,128]{2,0,1:T(8,128)(2,1)S(1)}, ...), branch_computations={%region_7.7_spmd, %region_8.8_spmd} | conditional | flops 405832448 | bytes 8564814 | solution.py:106
  369.3 1.5 subtract_exponential_fusion
  372.2 1.8 fusion.30
  374.7 4.9 %conditional.7 = ((f32[256,3,128]{0,2,1:T(8,128)S(1)}, f32[256,3,128]{0,2,1:T(8,128)S(1)})) conditional(s32[]{:T(128)} %convert_element_type.71, (f32[256,3,128]{0,2,1:T(8,128)S(1)}, f32[256,3,128]{0,2,1:T(8,128)S(1)}) %tuple.108, (s32[]{:T(128)}, bf16[8192,3,128]{2,0,1:T(8,128)(2,1)}, s32[]{:T(128)}, bf16[256,3,128]{2,0,1:T(8,128)(2,1)S(1)}, ...), branch_computations={%region_7.7_spmd, %region_8.8_spmd} | conditional | flops 405832448 | bytes 8564814 | solution.py:106
  374.9 1.5 subtract_exponential_fusion
  377.8 1.8 fusion.30
  380.3 4.9 %conditional.7 = ((f32[256,3,128]{0,2,1:T(8,128)S(1)}, f32[256,3,128]{0,2,1:T(8,128)S(1)})) conditional(s32[]{:T(128)} %convert_element_type.71, (f32[256,3,128]{0,2,1:T(8,128)S(1)}, f32[256,3,128]{0,2,1:T(8,128)S(1)}) %tuple.108, (s32[]{:T(128)}, bf16[8192,3,128]{2,0,1:T(8,128)(2,1)}, s32[]{:T(128)}, bf16[256,3,128]{2,0,1:T(8,128)(2,1)S(1)}, ...), branch_computations={%region_7.7_spmd, %region_8.8_spmd} | conditional | flops 405832448 | bytes 8564814 | solution.py:106
  380.5 1.5 subtract_exponential_fusion
  383.4 1.8 fusion.30
  385.9 4.9 %conditional.7 = ((f32[256,3,128]{0,2,1:T(8,128)S(1)}, f32[256,3,128]{0,2,1:T(8,128)S(1)})) conditional(s32[]{:T(128)} %convert_element_type.71, (f32[256,3,128]{0,2,1:T(8,128)S(1)}, f32[256,3,128]{0,2,1:T(8,128)S(1)}) %tuple.108, (s32[]{:T(128)}, bf16[8192,3,128]{2,0,1:T(8,128)(2,1)}, s32[]{:T(128)}, bf16[256,3,128]{2,0,1:T(8,128)(2,1)S(1)}, ...), branch_computations={%region_7.7_spmd, %region_8.8_spmd} | conditional | flops 405832448 | bytes 8564814 | solution.py:106
  386.1 1.5 subtract_exponential_fusion
  389.0 1.8 fusion.30
  391.5 4.9 %conditional.7 = ((f32[256,3,128]{0,2,1:T(8,128)S(1)}, f32[256,3,128]{0,2,1:T(8,128)S(1)})) conditional(s32[]{:T(128)} %convert_element_type.71, (f32[256,3,128]{0,2,1:T(8,128)S(1)}, f32[256,3,128]{0,2,1:T(8,128)S(1)}) %tuple.108, (s32[]{:T(128)}, bf16[8192,3,128]{2,0,1:T(8,128)(2,1)}, s32[]{:T(128)}, bf16[256,3,128]{2,0,1:T(8,128)(2,1)S(1)}, ...), branch_computations={%region_7.7_spmd, %region_8.8_spmd} | conditional | flops 405832448 | bytes 8564814 | solution.py:106
  391.7 1.5 subtract_exponential_fusion
  393.2 1.4 fusion.27
  394.6 1.8 fusion.30
  397.1 4.9 %conditional.7 = ((f32[256,3,128]{0,2,1:T(8,128)S(1)}, f32[256,3,128]{0,2,1:T(8,128)S(1)})) conditional(s32[]{:T(128)} %convert_element_type.71, (f32[256,3,128]{0,2,1:T(8,128)S(1)}, f32[256,3,128]{0,2,1:T(8,128)S(1)}) %tuple.108, (s32[]{:T(128)}, bf16[8192,3,128]{2,0,1:T(8,128)(2,1)}, s32[]{:T(128)}, bf16[256,3,128]{2,0,1:T(8,128)(2,1)S(1)}, ...), branch_computations={%region_7.7_spmd, %region_8.8_spmd} | conditional | flops 405832448 | bytes 8564814 | solution.py:106
  397.3 1.5 subtract_exponential_fusion
  400.2 1.8 fusion.30
  402.6 4.9 %conditional.7 = ((f32[256,3,128]{0,2,1:T(8,128)S(1)}, f32[256,3,128]{0,2,1:T(8,128)S(1)})) conditional(s32[]{:T(128)} %convert_element_type.71, (f32[256,3,128]{0,2,1:T(8,128)S(1)}, f32[256,3,128]{0,2,1:T(8,128)S(1)}) %tuple.108, (s32[]{:T(128)}, bf16[8192,3,128]{2,0,1:T(8,128)(2,1)}, s32[]{:T(128)}, bf16[256,3,128]{2,0,1:T(8,128)(2,1)S(1)}, ...), branch_computations={%region_7.7_spmd, %region_8.8_spmd} | conditional | flops 405832448 | bytes 8564814 | solution.py:106
  402.9 1.5 subtract_exponential_fusion
  404.4 1.4 fusion.27
  405.8 1.8 fusion.30
  408.2 4.9 %conditional.7 = ((f32[256,3,128]{0,2,1:T(8,128)S(1)}, f32[256,3,128]{0,2,1:T(8,128)S(1)})) conditional(s32[]{:T(128)} %convert_element_type.71, (f32[256,3,128]{0,2,1:T(8,128)S(1)}, f32[256,3,128]{0,2,1:T(8,128)S(1)}) %tuple.108, (s32[]{:T(128)}, bf16[8192,3,128]{2,0,1:T(8,128)(2,1)}, s32[]{:T(128)}, bf16[256,3,128]{2,0,1:T(8,128)(2,1)S(1)}, ...), branch_computations={%region_7.7_spmd, %region_8.8_spmd} | conditional | flops 405832448 | bytes 8564814 | solution.py:106
  408.5 1.5 subtract_exponential_fusion
  411.4 1.8 fusion.30
  413.8 4.9 %conditional.7 = ((f32[256,3,128]{0,2,1:T(8,128)S(1)}, f32[256,3,128]{0,2,1:T(8,128)S(1)})) conditional(s32[]{:T(128)} %convert_element_type.71, (f32[256,3,128]{0,2,1:T(8,128)S(1)}, f32[256,3,128]{0,2,1:T(8,128)S(1)}) %tuple.108, (s32[]{:T(128)}, bf16[8192,3,128]{2,0,1:T(8,128)(2,1)}, s32[]{:T(128)}, bf16[256,3,128]{2,0,1:T(8,128)(2,1)S(1)}, ...), branch_computations={%region_7.7_spmd, %region_8.8_spmd} | conditional | flops 405832448 | bytes 8564814 | solution.py:106
  414.0 1.5 subtract_exponential_fusion
  415.6 1.4 fusion.27
  416.9 1.8 fusion.30
  419.4 4.9 %conditional.7 = ((f32[256,3,128]{0,2,1:T(8,128)S(1)}, f32[256,3,128]{0,2,1:T(8,128)S(1)})) conditional(s32[]{:T(128)} %convert_element_type.71, (f32[256,3,128]{0,2,1:T(8,128)S(1)}, f32[256,3,128]{0,2,1:T(8,128)S(1)}) %tuple.108, (s32[]{:T(128)}, bf16[8192,3,128]{2,0,1:T(8,128)(2,1)}, s32[]{:T(128)}, bf16[256,3,128]{2,0,1:T(8,128)(2,1)S(1)}, ...), branch_computations={%region_7.7_spmd, %region_8.8_spmd} | conditional | flops 405832448 | bytes 8564814 | solution.py:106
  419.6 1.5 subtract_exponential_fusion
  422.5 1.8 fusion.30
  425.0 4.9 %conditional.7 = ((f32[256,3,128]{0,2,1:T(8,128)S(1)}, f32[256,3,128]{0,2,1:T(8,128)S(1)})) conditional(s32[]{:T(128)} %convert_element_type.71, (f32[256,3,128]{0,2,1:T(8,128)S(1)}, f32[256,3,128]{0,2,1:T(8,128)S(1)}) %tuple.108, (s32[]{:T(128)}, bf16[8192,3,128]{2,0,1:T(8,128)(2,1)}, s32[]{:T(128)}, bf16[256,3,128]{2,0,1:T(8,128)(2,1)S(1)}, ...), branch_computations={%region_7.7_spmd, %region_8.8_spmd} | conditional | flops 405832448 | bytes 8564814 | solution.py:106
  425.2 1.5 subtract_exponential_fusion
  426.8 1.4 fusion.27
  428.1 1.8 fusion.30
  430.6 4.9 %conditional.7 = ((f32[256,3,128]{0,2,1:T(8,128)S(1)}, f32[256,3,128]{0,2,1:T(8,128)S(1)})) conditional(s32[]{:T(128)} %convert_element_type.71, (f32[256,3,128]{0,2,1:T(8,128)S(1)}, f32[256,3,128]{0,2,1:T(8,128)S(1)}) %tuple.108, (s32[]{:T(128)}, bf16[8192,3,128]{2,0,1:T(8,128)(2,1)}, s32[]{:T(128)}, bf16[256,3,128]{2,0,1:T(8,128)(2,1)S(1)}, ...), branch_computations={%region_7.7_spmd, %region_8.8_spmd} | conditional | flops 405832448 | bytes 8564814 | solution.py:106
  430.8 1.5 subtract_exponential_fusion
  433.7 1.8 fusion.30
  436.2 4.9 %conditional.7 = ((f32[256,3,128]{0,2,1:T(8,128)S(1)}, f32[256,3,128]{0,2,1:T(8,128)S(1)})) conditional(s32[]{:T(128)} %convert_element_type.71, (f32[256,3,128]{0,2,1:T(8,128)S(1)}, f32[256,3,128]{0,2,1:T(8,128)S(1)}) %tuple.108, (s32[]{:T(128)}, bf16[8192,3,128]{2,0,1:T(8,128)(2,1)}, s32[]{:T(128)}, bf16[256,3,128]{2,0,1:T(8,128)(2,1)S(1)}, ...), branch_computations={%region_7.7_spmd, %region_8.8_spmd} | conditional | flops 405832448 | bytes 8564814 | solution.py:106
  436.4 1.5 subtract_exponential_fusion
  439.3 1.8 fusion.30
  441.8 4.9 %conditional.7 = ((f32[256,3,128]{0,2,1:T(8,128)S(1)}, f32[256,3,128]{0,2,1:T(8,128)S(1)})) conditional(s32[]{:T(128)} %convert_element_type.71, (f32[256,3,128]{0,2,1:T(8,128)S(1)}, f32[256,3,128]{0,2,1:T(8,128)S(1)}) %tuple.108, (s32[]{:T(128)}, bf16[8192,3,128]{2,0,1:T(8,128)(2,1)}, s32[]{:T(128)}, bf16[256,3,128]{2,0,1:T(8,128)(2,1)S(1)}, ...), branch_computations={%region_7.7_spmd, %region_8.8_spmd} | conditional | flops 405832448 | bytes 8564814 | solution.py:106
  442.0 1.5 subtract_exponential_fusion
  444.9 1.8 fusion.30
  447.3 4.9 %conditional.7 = ((f32[256,3,128]{0,2,1:T(8,128)S(1)}, f32[256,3,128]{0,2,1:T(8,128)S(1)})) conditional(s32[]{:T(128)} %convert_element_type.71, (f32[256,3,128]{0,2,1:T(8,128)S(1)}, f32[256,3,128]{0,2,1:T(8,128)S(1)}) %tuple.108, (s32[]{:T(128)}, bf16[8192,3,128]{2,0,1:T(8,128)(2,1)}, s32[]{:T(128)}, bf16[256,3,128]{2,0,1:T(8,128)(2,1)S(1)}, ...), branch_computations={%region_7.7_spmd, %region_8.8_spmd} | conditional | flops 405832448 | bytes 8564814 | solution.py:106
  447.6 1.5 subtract_exponential_fusion
  450.5 1.8 fusion.30
  452.9 4.9 %conditional.7 = ((f32[256,3,128]{0,2,1:T(8,128)S(1)}, f32[256,3,128]{0,2,1:T(8,128)S(1)})) conditional(s32[]{:T(128)} %convert_element_type.71, (f32[256,3,128]{0,2,1:T(8,128)S(1)}, f32[256,3,128]{0,2,1:T(8,128)S(1)}) %tuple.108, (s32[]{:T(128)}, bf16[8192,3,128]{2,0,1:T(8,128)(2,1)}, s32[]{:T(128)}, bf16[256,3,128]{2,0,1:T(8,128)(2,1)S(1)}, ...), branch_computations={%region_7.7_spmd, %region_8.8_spmd} | conditional | flops 405832448 | bytes 8564814 | solution.py:106
  453.2 1.5 subtract_exponential_fusion
  456.1 1.8 fusion.30
  (160 shorter events, 30.4 us)
Async XLA Ops:
  7.2 69.4 %all-gather.10.cloned.1.call-start = ((), (), s32[]{:S(2)}) async-start(), calls=%async_computation.2 | async-start | bytes 2949120 | tf_op jit(solution)/shard_map/all_gather | solution.py:123
  7.9 145.1 %all-gather.6.cloned.1.call-start = ((), (), s32[]{:S(2)}) async-start(), calls=%async_computation | async-start | bytes 6488064 | tf_op jit(solution)/shard_map/all_gather | solution.py:135
  8.6 208.7 %all-gather.8.cloned.1.call-start = ((), (), s32[]{:S(2)}) async-start(), calls=%async_computation.1 | async-start | bytes 6488064 | tf_op jit(solution)/shard_map/all_gather | solution.py:136
  9.4 74.4 %copy-start.4 = (f32[256,3]{0,1:T(4,128)S(1)}, f32[256,3]{0,1:T(4,128)}, u32[]{:S(2)}) copy-start(f32[256,3]{0,1:T(4,128)} %param.21) | copy-start | bytes 9220
  9.4 289.7 %all-gather.14.cloned.1.call-start = ((), (), s32[]{:S(2)}) async-start(), calls=%async_computation.4 | async-start | bytes 6488064 | tf_op jit(solution)/shard_map/all_gather | solution.py:144
  81.0 40.6 %copy-start.3 = (bf16[256,3,128]{2,0,1:T(8,128)(2,1)S(1)}, bf16[256,3,128]{2,0,1:T(8,128)(2,1)}, u32[]{:S(2)}) copy-start(bf16[256,3,128]{2,0,1:T(8,128)(2,1)} %param.18) | copy-start | bytes 589828
  81.0 136.4 %copy-start = (bf16[256,3,128]{2,0,1:T(8,128)(2,1)S(1)}, bf16[256,3,128]{2,0,1:T(8,128)(2,1)}, u32[]{:S(2)}) copy-start(bf16[256,3,128]{2,0,1:T(8,128)(2,1)} %param.15) | copy-start | bytes 589828
  81.9 286.5 %all-gather.12.cloned.1.call-start = ((), (), s32[]{:S(2)}) async-start(), calls=%async_computation.3 | async-start | bytes 6488064 | tf_op jit(solution)/shard_map/all_gather | solution.py:143
  232.9 135.6 %copy-start.1 = (bf16[256,3,128]{2,0,1:T(8,128)(2,1)S(1)}, bf16[256,3,128]{2,0,1:T(8,128)(2,1)}, u32[]{:S(2)}) copy-start(bf16[256,3,128]{2,0,1:T(8,128)(2,1)} %param.17) | copy-start | bytes 589828
  232.9 135.6 %copy-start.2 = (bf16[256,3,128]{2,0,1:T(8,128)(2,1)S(1)}, bf16[256,3,128]{2,0,1:T(8,128)(2,1)}, u32[]{:S(2)}) copy-start(bf16[256,3,128]{2,0,1:T(8,128)(2,1)} %param.16) | copy-start | bytes 589828
Sparse Core Ops, SparseCore 0:
  10.7 65.8 all-gather.9
  78.5 68.2 all-gather.5
  148.6 68.7 all-gather.7
  219.6 79.4 all-gather.13
  300.8 67.5 all-gather.11
where the time goes:
time: 468 us; the launch traced here: 466 us
  waiting for transfers between devices  261 us (56%)
  matrix products  82.6 us (18%)
  blocking collectives  66.8 us (14%)
  loops' own time  23 us (5%)
  local copies, waits for them, and re-layouts  14.4 us (3%)
  between operations  13.9 us (3%)
    all_gather x1, waiting for transfers between devices, body(): lax.all_gather(output_grad, 'head', axis=1, tiled=True)  67.1 us
    all_gather x1, waiting for transfers between devices, body(): lax.all_gather(attn_grad, 'ctx', axis=0, tiled=True)  66.2 us
    all_gather x1, waiting for transfers between devices, body(): lax.all_gather(value_vectors, 'ctx', axis=0, tiled=True)  64.4 us
    all_gather x1, waiting for transfers between devices, body(): lax.all_gather(queries, 'ctx', axis=0, tiled=True)  60.7 us
    all_gather x1, blocking collectives, body(): lax.all_gather(own_total, 'ctx', axis=1, tiled=True)  35.6 us
    all_gather x1, blocking collectives, body(): lax.all_gather(row_delta, 'ctx', axis=1, tiled=True)  31.2 us
    dot_general x16, matrix products, key_update(): jnp.einsum('hqk,qhd->khd', score_grad, query_block, preferred_element_typ...  28.6 us
    dot_general x17, matrix products, block_terms(): jnp.einsum('qhd,khd->hqk', query_block, key_block, preferred_element_type...  25.9 us
  transfers between devices with their start and end apart: 5, of which 4 were waited for; matrix products, arithmetic and copies ran while one was open for 5% of the time, Pallas kernels for 0%

commit v1 on v0

--- a/solution.py
+++ b/solution.py
@@ -120,7 +120,9 @@
     span_rows = min(512, total_len)
     grad_flat = jnp.einsum(
         "tc,rc->tr",
-        lax.all_gather(output_grad, "head", axis=1, tiled=True),
+        jnp.concatenate(
+            lax.all_to_all(jnp.stack([output_grad] * lax.axis_size("head")), "head", 0, 0), axis=1
+        ),
         w_out,
         preferred_element_type=jnp.float32,
     )

time: 468 us -> 411 us (0.88)
  waiting for transfers between devices: 261 us -> 138 us
  blocking collectives: 66.8 us -> 134 us
    all_gather x1 -> x0, waiting for transfers between devices: 67.1 us -> none  [body(): lax.all_gather(output_grad, 'head', axis=1, tiled=True)]
    all_to_all x0 -> x1, blocking collectives: none -> 58.8 us  [body(): lax.all_to_all(jnp.stack([output_grad] * lax.axis_size('head')), 'head',...]
    all_gather x1, waiting for transfers between devices: 64.4 us -> 8.47 us  [body(): lax.all_gather(value_vectors, 'ctx', axis=0, tiled=True)]
    all_gather x1, blocking collectives: 35.6 us -> 44.1 us  [body(): lax.all_gather(own_total, 'ctx', axis=1, tiled=True)]
    unnamed x13 -> x16, local copies, waits for them, and re-layouts: 10.8 us -> 11.9 us
  transfers between devices with their start and end apart: 5 -> 4, of which waited for: 4 -> 3; matrix products, arithmetic and copies ran while one was open for 5% -> 5% of each run, Pallas kernels for 0% -> 0%
where the time goes in v1:
time: 411 us; the launch traced here: 408 us
  waiting for transfers between devices  138 us (34%)
  blocking collectives  134 us (33%)
  matrix products  80 us (19%)
  loops' own time  22.7 us (6%)
  local copies, waits for them, and re-layouts  15.7 us (4%)
  between operations  13.9 us (3%)
    all_gather x1, waiting for transfers between devices, body(): lax.all_gather(attn_grad, 'ctx', axis=0, tiled=True)  66.3 us
    all_gather x1, waiting for transfers between devices, body(): lax.all_gather(queries, 'ctx', axis=0, tiled=True)  61 us
    all_to_all x1, blocking collectives, body(): lax.all_to_all(jnp.stack([output_grad] * lax.axis_size('head')), 'head',...  58.8 us
    all_gather x1, blocking collectives, body(): lax.all_gather(own_total, 'ctx', axis=1, tiled=True)  44.1 us
    all_gather x1, blocking collectives, body(): lax.all_gather(row_delta, 'ctx', axis=1, tiled=True)  31.2 us
    dot_general x16, matrix products, key_update(): jnp.einsum('hqk,qhd->khd', score_grad, query_block, preferred_element_typ...  28.8 us
    dot_general x17, matrix products, block_terms(): jnp.einsum('qhd,khd->hqk', query_block, key_block, preferred_element_type...  25.8 us
    dot_general x16, matrix products, key_update(): jnp.einsum('hqk,qhd->khd', prob_low, grad_block, preferred_element_type=j...  21.8 us
  transfers between devices with their start and end apart: 4, of which 3 were waited for; matrix products, arithmetic and copies ran while one was open for 5% of the time, Pallas kernels for 0%

profile of v1, /device:TPU:1, one launch (start us, length us, event | category | flops | bytes accessed | tf_op | source)
XLA Modules:
  0.0 408.4 jit_solution(1738876588022447413)
XLA Ops:
  10.0 58.8 %all_to_all.5 = bf16[8,256,640]{1,2,0:T(8,128)(2,1)S(1)} all-to-all(bf16[8,256,640]{1,2,0:T(8,128)(2,1)S(1)} %stack.2), channel_id=1, replica_groups=mesh['ctx'=32,'head'=8] {'head'}, dimensions={0} | all-to-all | bytes 5242880 | tf_op jit(solution)/shard_map/all_to_all | solution.py:124
  68.9 1.6 convolution_convert_fusion
  73.2 44.1 %all_gather.21 = f32[3,8192]{1,0:T(4,128)S(1)} all-gather(f32[3,256]{1,0:T(4,128)S(1)} %bitcast.60), channel_id=1, replica_groups=mesh['ctx'=32,'head'=8] {'ctx'}, dimensions={1}, use_global_device_ids=true | all-gather | bytes 101376 | tf_op jit(solution)/shard_map/all_gather | solution.py:149
  119.7 31.2 %all_gather.23 = f32[3,8192]{1,0:T(4,128)S(1)} all-gather(f32[3,256]{1,0:T(4,128)S(1)} %multiply_reduce_fusion), channel_id=1, replica_groups=mesh['ctx'=32,'head'=8] {'ctx'}, dimensions={1}, use_global_device_ids=true | all-gather | bytes 101376 | tf_op jit(solution)/shard_map/all_gather | solution.py:150
  150.9 8.5 %all-gather.7.cloned.1.call-done = bf16[8192,3,128]{2,0,1:T(8,128)(2,1)} async-done(((bf16[256,3,128]{2,0,1:T(8,128)(2,1)}), bf16[8192,3,128]{2,0,1:T(8,128)(2,1)}) %all-gather.7.cloned.1.call-update) | async-done | bytes 6291472 | tf_op jit(solution)/shard_map/all_gather | solution.py:138
  159.4 14.6 %while.37 = (s32[]{:T(128)}, f32[256,3,128]{0,2,1:T(8,128)S(1)}, s32[]{:T(128)}, bf16[8192,3,128]{2,0,1:T(8,128)(2,1)}, bf16[256,3,128]{2,0,1:T(8,128)(2,1)S(1)}...) while((s32[]{:T(128)}, f32[256,3,128]{0,2,1:T(8,128)S(1)}, ...), condition=%wide.region_4.5_spmd.clone, body=%wide.region_1.4_spmd.clone.sunk | while | flops 304677632 | bytes 5782805 | solution.py:65
  160.1 3.5 conditional.6
  160.1 1.4 fusion.19
  161.7 1.9 fusion.10
  174.9 66.3 %all-gather.11.cloned.1.call-done = bf16[8192,3,128]{0,2,1:T(8,128)(2,1)} async-done(((bf16[256,3,128]{0,2,1:T(8,128)(2,1)}), bf16[8192,3,128]{0,2,1:T(8,128)(2,1)}) %all-gather.11.cloned.1.call-update) | async-done | bytes 6291472 | tf_op jit(solution)/shard_map/all_gather | solution.py:146
  241.2 8.6 %copy.38 = bf16[8192,3,128]{2,0,1:T(8,128)(2,1)} copy(bf16[8192,3,128]{0,2,1:T(8,128)(2,1)} %all-gather.11.cloned.1.call-done) | data formatting | bytes 12582912
  249.8 61.0 %all-gather.9.cloned.1.call-done = bf16[8192,3,128]{2,0,1:T(8,128)(2,1)} async-done(((bf16[256,3,128]{2,0,1:T(8,128)(2,1)}), bf16[8192,3,128]{2,0,1:T(8,128)(2,1)}) %all-gather.9.cloned.1.call-update) | async-done | bytes 6291472 | tf_op jit(solution)/shard_map/all_gather | solution.py:145
  310.9 89.3 %while.38 = (s32[]{:T(128)}, f32[256,3,128]{0,2,1:T(8,128)S(1)}, f32[256,3,128]{0,2,1:T(8,128)S(1)}, s32[]{:T(128)}, bf16[8192,3,128]{2,0,1:T(8,128)(2,1)}, /*in...) while((s32[]{:T(128)}, f32[256,3,128]{0,2,1:T(8,128)S(1)}, ...), condition=%wide.region_9.10_spmd.clone, body=%wide.region_6.9_spmd.clone.sunk | while | flops 405832448 | bytes 8566113 | solution.py:111
  311.5 4.9 %conditional.7 = ((f32[256,3,128]{0,2,1:T(8,128)S(1)}, f32[256,3,128]{0,2,1:T(8,128)S(1)})) conditional(s32[]{:T(128)} %convert_element_type.71, (f32[256,3,128]{0,2,1:T(8,128)S(1)}, f32[256,3,128]{0,2,1:T(8,128)S(1)}) %tuple.108, (s32[]{:T(128)}, bf16[8192,3,128]{2,0,1:T(8,128)(2,1)}, s32[]{:T(128)}, bf16[256,3,128]{2,0,1:T(8,128)(2,1)S(1)}, ...), branch_computations={%region_7.7_spmd, %region_8.8_spmd} | conditional | flops 405832448 | bytes 8564814 | solution.py:106
  311.8 1.5 subtract_exponential_fusion
  314.7 1.8 fusion.30
  317.1 4.9 %conditional.7 = ((f32[256,3,128]{0,2,1:T(8,128)S(1)}, f32[256,3,128]{0,2,1:T(8,128)S(1)})) conditional(s32[]{:T(128)} %convert_element_type.71, (f32[256,3,128]{0,2,1:T(8,128)S(1)}, f32[256,3,128]{0,2,1:T(8,128)S(1)}) %tuple.108, (s32[]{:T(128)}, bf16[8192,3,128]{2,0,1:T(8,128)(2,1)}, s32[]{:T(128)}, bf16[256,3,128]{2,0,1:T(8,128)(2,1)S(1)}, ...), branch_computations={%region_7.7_spmd, %region_8.8_spmd} | conditional | flops 405832448 | bytes 8564814 | solution.py:106
  317.3 1.5 subtract_exponential_fusion
  320.2 1.8 fusion.30
  322.7 4.9 %conditional.7 = ((f32[256,3,128]{0,2,1:T(8,128)S(1)}, f32[256,3,128]{0,2,1:T(8,128)S(1)})) conditional(s32[]{:T(128)} %convert_element_type.71, (f32[256,3,128]{0,2,1:T(8,128)S(1)}, f32[256,3,128]{0,2,1:T(8,128)S(1)}) %tuple.108, (s32[]{:T(128)}, bf16[8192,3,128]{2,0,1:T(8,128)(2,1)}, s32[]{:T(128)}, bf16[256,3,128]{2,0,1:T(8,128)(2,1)S(1)}, ...), branch_computations={%region_7.7_spmd, %region_8.8_spmd} | conditional | flops 405832448 | bytes 8564814 | solution.py:106
  322.9 1.5 subtract_exponential_fusion
  325.8 1.8 fusion.30
  328.3 4.9 %conditional.7 = ((f32[256,3,128]{0,2,1:T(8,128)S(1)}, f32[256,3,128]{0,2,1:T(8,128)S(1)})) conditional(s32[]{:T(128)} %convert_element_type.71, (f32[256,3,128]{0,2,1:T(8,128)S(1)}, f32[256,3,128]{0,2,1:T(8,128)S(1)}) %tuple.108, (s32[]{:T(128)}, bf16[8192,3,128]{2,0,1:T(8,128)(2,1)}, s32[]{:T(128)}, bf16[256,3,128]{2,0,1:T(8,128)(2,1)S(1)}, ...), branch_computations={%region_7.7_spmd, %region_8.8_spmd} | conditional | flops 405832448 | bytes 8564814 | solution.py:106
  328.5 1.5 subtract_exponential_fusion
  331.4 1.8 fusion.30
  333.9 4.9 %conditional.7 = ((f32[256,3,128]{0,2,1:T(8,128)S(1)}, f32[256,3,128]{0,2,1:T(8,128)S(1)})) conditional(s32[]{:T(128)} %convert_element_type.71, (f32[256,3,128]{0,2,1:T(8,128)S(1)}, f32[256,3,128]{0,2,1:T(8,128)S(1)}) %tuple.108, (s32[]{:T(128)}, bf16[8192,3,128]{2,0,1:T(8,128)(2,1)}, s32[]{:T(128)}, bf16[256,3,128]{2,0,1:T(8,128)(2,1)S(1)}, ...), branch_computations={%region_7.7_spmd, %region_8.8_spmd} | conditional | flops 405832448 | bytes 8564814 | solution.py:106
  334.1 1.5 subtract_exponential_fusion
  335.6 1.4 fusion.27
  337.0 1.8 fusion.30
  339.4 4.9 %conditional.7 = ((f32[256,3,128]{0,2,1:T(8,128)S(1)}, f32[256,3,128]{0,2,1:T(8,128)S(1)})) conditional(s32[]{:T(128)} %convert_element_type.71, (f32[256,3,128]{0,2,1:T(8,128)S(1)}, f32[256,3,128]{0,2,1:T(8,128)S(1)}) %tuple.108, (s32[]{:T(128)}, bf16[8192,3,128]{2,0,1:T(8,128)(2,1)}, s32[]{:T(128)}, bf16[256,3,128]{2,0,1:T(8,128)(2,1)S(1)}, ...), branch_computations={%region_7.7_spmd, %region_8.8_spmd} | conditional | flops 405832448 | bytes 8564814 | solution.py:106
  339.7 1.5 subtract_exponential_fusion
  341.2 1.4 fusion.27
  342.6 1.8 fusion.30
  345.0 4.9 %conditional.7 = ((f32[256,3,128]{0,2,1:T(8,128)S(1)}, f32[256,3,128]{0,2,1:T(8,128)S(1)})) conditional(s32[]{:T(128)} %convert_element_type.71, (f32[256,3,128]{0,2,1:T(8,128)S(1)}, f32[256,3,128]{0,2,1:T(8,128)S(1)}) %tuple.108, (s32[]{:T(128)}, bf16[8192,3,128]{2,0,1:T(8,128)(2,1)}, s32[]{:T(128)}, bf16[256,3,128]{2,0,1:T(8,128)(2,1)S(1)}, ...), branch_computations={%region_7.7_spmd, %region_8.8_spmd} | conditional | flops 405832448 | bytes 8564814 | solution.py:106
  345.2 1.5 subtract_exponential_fusion
  348.1 1.8 fusion.30
  350.6 4.9 %conditional.7 = ((f32[256,3,128]{0,2,1:T(8,128)S(1)}, f32[256,3,128]{0,2,1:T(8,128)S(1)})) conditional(s32[]{:T(128)} %convert_element_type.71, (f32[256,3,128]{0,2,1:T(8,128)S(1)}, f32[256,3,128]{0,2,1:T(8,128)S(1)}) %tuple.108, (s32[]{:T(128)}, bf16[8192,3,128]{2,0,1:T(8,128)(2,1)}, s32[]{:T(128)}, bf16[256,3,128]{2,0,1:T(8,128)(2,1)S(1)}, ...), branch_computations={%region_7.7_spmd, %region_8.8_spmd} | conditional | flops 405832448 | bytes 8564814 | solution.py:106
  350.8 1.5 subtract_exponential_fusion
  353.7 1.8 fusion.30
  356.2 4.9 %conditional.7 = ((f32[256,3,128]{0,2,1:T(8,128)S(1)}, f32[256,3,128]{0,2,1:T(8,128)S(1)})) conditional(s32[]{:T(128)} %convert_element_type.71, (f32[256,3,128]{0,2,1:T(8,128)S(1)}, f32[256,3,128]{0,2,1:T(8,128)S(1)}) %tuple.108, (s32[]{:T(128)}, bf16[8192,3,128]{2,0,1:T(8,128)(2,1)}, s32[]{:T(128)}, bf16[256,3,128]{2,0,1:T(8,128)(2,1)S(1)}, ...), branch_computations={%region_7.7_spmd, %region_8.8_spmd} | conditional | flops 405832448 | bytes 8564814 | solution.py:106
  356.4 1.5 subtract_exponential_fusion
  359.3 1.8 fusion.30
  361.8 4.9 %conditional.7 = ((f32[256,3,128]{0,2,1:T(8,128)S(1)}, f32[256,3,128]{0,2,1:T(8,128)S(1)})) conditional(s32[]{:T(128)} %convert_element_type.71, (f32[256,3,128]{0,2,1:T(8,128)S(1)}, f32[256,3,128]{0,2,1:T(8,128)S(1)}) %tuple.108, (s32[]{:T(128)}, bf16[8192,3,128]{2,0,1:T(8,128)(2,1)}, s32[]{:T(128)}, bf16[256,3,128]{2,0,1:T(8,128)(2,1)S(1)}, ...), branch_computations={%region_7.7_spmd, %region_8.8_spmd} | conditional | flops 405832448 | bytes 8564814 | solution.py:106
  362.0 1.5 subtract_exponential_fusion
  364.9 1.8 fusion.30
  367.4 4.9 %conditional.7 = ((f32[256,3,128]{0,2,1:T(8,128)S(1)}, f32[256,3,128]{0,2,1:T(8,128)S(1)})) conditional(s32[]{:T(128)} %convert_element_type.71, (f32[256,3,128]{0,2,1:T(8,128)S(1)}, f32[256,3,128]{0,2,1:T(8,128)S(1)}) %tuple.108, (s32[]{:T(128)}, bf16[8192,3,128]{2,0,1:T(8,128)(2,1)}, s32[]{:T(128)}, bf16[256,3,128]{2,0,1:T(8,128)(2,1)S(1)}, ...), branch_computations={%region_7.7_spmd, %region_8.8_spmd} | conditional | flops 405832448 | bytes 8564814 | solution.py:106
  367.6 1.5 subtract_exponential_fusion
  370.5 1.8 fusion.30
  372.9 4.9 %conditional.7 = ((f32[256,3,128]{0,2,1:T(8,128)S(1)}, f32[256,3,128]{0,2,1:T(8,128)S(1)})) conditional(s32[]{:T(128)} %convert_element_type.71, (f32[256,3,128]{0,2,1:T(8,128)S(1)}, f32[256,3,128]{0,2,1:T(8,128)S(1)}) %tuple.108, (s32[]{:T(128)}, bf16[8192,3,128]{2,0,1:T(8,128)(2,1)}, s32[]{:T(128)}, bf16[256,3,128]{2,0,1:T(8,128)(2,1)S(1)}, ...), branch_computations={%region_7.7_spmd, %region_8.8_spmd} | conditional | flops 405832448 | bytes 8564814 | solution.py:106
  373.2 1.5 subtract_exponential_fusion
  376.1 1.8 fusion.30
  378.5 4.9 %conditional.7 = ((f32[256,3,128]{0,2,1:T(8,128)S(1)}, f32[256,3,128]{0,2,1:T(8,128)S(1)})) conditional(s32[]{:T(128)} %convert_element_type.71, (f32[256,3,128]{0,2,1:T(8,128)S(1)}, f32[256,3,128]{0,2,1:T(8,128)S(1)}) %tuple.108, (s32[]{:T(128)}, bf16[8192,3,128]{2,0,1:T(8,128)(2,1)}, s32[]{:T(128)}, bf16[256,3,128]{2,0,1:T(8,128)(2,1)S(1)}, ...), branch_computations={%region_7.7_spmd, %region_8.8_spmd} | conditional | flops 405832448 | bytes 8564814 | solution.py:106
  378.7 1.5 subtract_exponential_fusion
  381.6 1.8 fusion.30
  384.1 4.9 %conditional.7 = ((f32[256,3,128]{0,2,1:T(8,128)S(1)}, f32[256,3,128]{0,2,1:T(8,128)S(1)})) conditional(s32[]{:T(128)} %convert_element_type.71, (f32[256,3,128]{0,2,1:T(8,128)S(1)}, f32[256,3,128]{0,2,1:T(8,128)S(1)}) %tuple.108, (s32[]{:T(128)}, bf16[8192,3,128]{2,0,1:T(8,128)(2,1)}, s32[]{:T(128)}, bf16[256,3,128]{2,0,1:T(8,128)(2,1)S(1)}, ...), branch_computations={%region_7.7_spmd, %region_8.8_spmd} | conditional | flops 405832448 | bytes 8564814 | solution.py:106
  384.3 1.5 subtract_exponential_fusion
  385.9 1.4 fusion.27
  387.2 1.8 fusion.30
  389.7 4.9 %conditional.7 = ((f32[256,3,128]{0,2,1:T(8,128)S(1)}, f32[256,3,128]{0,2,1:T(8,128)S(1)})) conditional(s32[]{:T(128)} %convert_element_type.71, (f32[256,3,128]{0,2,1:T(8,128)S(1)}, f32[256,3,128]{0,2,1:T(8,128)S(1)}) %tuple.108, (s32[]{:T(128)}, bf16[8192,3,128]{2,0,1:T(8,128)(2,1)}, s32[]{:T(128)}, bf16[256,3,128]{2,0,1:T(8,128)(2,1)S(1)}, ...), branch_computations={%region_7.7_spmd, %region_8.8_spmd} | conditional | flops 405832448 | bytes 8564814 | solution.py:106
  389.9 1.5 subtract_exponential_fusion
  392.8 1.8 fusion.30
  395.3 4.9 %conditional.7 = ((f32[256,3,128]{0,2,1:T(8,128)S(1)}, f32[256,3,128]{0,2,1:T(8,128)S(1)})) conditional(s32[]{:T(128)} %convert_element_type.71, (f32[256,3,128]{0,2,1:T(8,128)S(1)}, f32[256,3,128]{0,2,1:T(8,128)S(1)}) %tuple.108, (s32[]{:T(128)}, bf16[8192,3,128]{2,0,1:T(8,128)(2,1)}, s32[]{:T(128)}, bf16[256,3,128]{2,0,1:T(8,128)(2,1)S(1)}, ...), branch_computations={%region_7.7_spmd, %region_8.8_spmd} | conditional | flops 405832448 | bytes 8564814 | solution.py:106
  395.5 1.5 subtract_exponential_fusion
  398.4 1.8 fusion.30
  (162 shorter events, 31.0 us)
Async XLA Ops:
  7.2 143.8 %all-gather.5.cloned.1.call-start = ((), (), s32[]{:S(2)}) async-start(), calls=%async_computation.1 | async-start | bytes 6488064 | tf_op jit(solution)/shard_map/all_gather | solution.py:137
  7.9 151.5 %all-gather.7.cloned.1.call-start = ((), (), s32[]{:S(2)}) async-start(), calls=%async_computation.2 | async-start | bytes 6488064 | tf_op jit(solution)/shard_map/all_gather | solution.py:138
  8.6 232.6 %all-gather.11.cloned.1.call-start = ((), (), s32[]{:S(2)}) async-start(), calls=%async_computation.4 | async-start | bytes 6488064 | tf_op jit(solution)/shard_map/all_gather | solution.py:146
  10.0 58.8 %copy-start.5 = (bf16[384,5120]{1,0:T(8,128)(2,1)S(1)}, bf16[384,5120]{1,0:T(8,128)(2,1)}, u32[]{:S(2)}) copy-start(bf16[384,5120]{1,0:T(8,128)(2,1)} %param.20) | copy-start | bytes 11796484
  68.9 4.3 %copy-start.4 = (f32[256,3]{0,1:T(4,128)S(1)}, f32[256,3]{0,1:T(4,128)}, u32[]{:S(2)}) copy-start(f32[256,3]{0,1:T(4,128)} %param.21) | copy-start | bytes 9220
  70.4 49.0 %copy-start.3 = (bf16[256,3,128]{2,0,1:T(8,128)(2,1)S(1)}, bf16[256,3,128]{2,0,1:T(8,128)(2,1)}, u32[]{:S(2)}) copy-start(bf16[256,3,128]{2,0,1:T(8,128)(2,1)} %param.18) | copy-start | bytes 589828
  70.5 89.0 %copy-start = (bf16[256,3,128]{2,0,1:T(8,128)(2,1)S(1)}, bf16[256,3,128]{2,0,1:T(8,128)(2,1)}, u32[]{:S(2)}) copy-start(bf16[256,3,128]{2,0,1:T(8,128)(2,1)} %param.15) | copy-start | bytes 589828
  71.3 239.5 %all-gather.9.cloned.1.call-start = ((), (), s32[]{:S(2)}) async-start(), calls=%async_computation.3 | async-start | bytes 6488064 | tf_op jit(solution)/shard_map/all_gather | solution.py:145
  174.9 136.0 %copy-start.1 = (bf16[256,3,128]{2,0,1:T(8,128)(2,1)S(1)}, bf16[256,3,128]{2,0,1:T(8,128)(2,1)}, u32[]{:S(2)}) copy-start(bf16[256,3,128]{2,0,1:T(8,128)(2,1)} %param.17) | copy-start | bytes 589828
  174.9 136.0 %copy-start.2 = (bf16[256,3,128]{2,0,1:T(8,128)(2,1)S(1)}, bf16[256,3,128]{2,0,1:T(8,128)(2,1)}, u32[]{:S(2)}) copy-start(bf16[256,3,128]{2,0,1:T(8,128)(2,1)} %param.16) | copy-start | bytes 589828
Sparse Core Ops, SparseCore 0:
  9.8 77.3 all-gather.4
  89.1 70.2 all-gather.6
  161.7 79.4 all-gather.10
  242.9 67.8 all-gather.8
